TPU v7x, 32 devices: a whole 2x2x4 slice. The times are simulated.
32 devices in a mesh: fsdp: 4 (over y, core), ctx: 8 (over z, x).
Axes of the slice: x: 2, y: 2, z: 4, core: 2. Of those that a mesh axis runs over, the one named last changes fastest.
Arguments:
- inputs: bfloat16 [4, 4096, 1536], P('fsdp', 'ctx'), may hold values from -8 to 8
- segment_ids: int32 [4, 4096], P('fsdp', 'ctx'), may hold values from 0 to 3, never falling along the last dimension, each value on 1 to 2048 neighbouring positions
- out_grad: bfloat16 [4, 4096, 1536], P('fsdp', 'ctx'), may hold values from -6 to 6
- in_matrix: bfloat16 [1536, 6448], P('fsdp'), may hold values from -0.15625 to 0.15625
- out_matrix: bfloat16 [3072, 1536], P('fsdp'), may hold values from -0.109375 to 0.109375
- conv_taps: bfloat16 [3328, 4], P('fsdp'), may hold values from -3 to 3
- conv_bias: bfloat16 [3328], P('fsdp'), may hold values from -2.5 to 2.5
- dt_bias: bfloat16 [48], P('fsdp'), may hold values from -6 to -2
- decay_log: bfloat16 [48], P('fsdp'), may hold values from -7 to 2.5
- skip_scale: bfloat16 [48], P('fsdp'), may hold values from 0.5 to 2
- mixer_gain: bfloat16 [3072], P('fsdp'), may hold values from 0.5 to 1.5
- input_gain: bfloat16 [1536], P('fsdp'), may hold values from 0.5 to 1.5
Outputs:
- block_out: bfloat16 [4, 4096, 1536], P('fsdp', 'ctx')
- input_grad: bfloat16 [4, 4096, 1536], P('fsdp', 'ctx')
- in_matrix_grad: float32 [1536, 6448], P('fsdp')
- out_matrix_grad: float32 [3072, 1536], P('fsdp')
- conv_taps_grad: float32 [3328, 4], P('fsdp')
- conv_bias_grad: float32 [3328], P('fsdp')
- dt_bias_grad: float32 [48], P('fsdp')
- decay_log_grad: float32 [48], P('fsdp')
- skip_scale_grad: float32 [48], P('fsdp')
- mixer_gain_grad: float32 [3072], P('fsdp')
- input_gain_grad: float32 [1536], P('fsdp')
- rms_stats: float32 [2], replicated
Inputs may be any that keep to these rules, and one draw needn't show every extreme that they name: `segment_ids`: along each sequence the numbers never fall; a run of equal numbers is one document; every number of 0 to 3 is used, and the longest document has exactly 2048 tokens.
All inputs are finite; a program needn't handle non-finite values.
Results may differ from a plain program's by a relative error of at most 0.015.
Values may be sent and summed in bfloat16 or wider, within the bound.
A program may use at most 320 MiB of HBM per device.

v0:
```python
import jax
import jax.numpy as jnp
from jax import lax
from jax.sharding import PartitionSpec as P

D = 1536
HEADS = 48
HDIM = 64
STATE = 128
CONV = 4
GROUP = 256
INNER = 3072
XBC = 3328
epsilon = 1e-05
precise = lax.Precision.HIGHEST


def passed_along(block, axis, distance):
    devices = range(lax.axis_size(axis))
    route = [(i - distance, i) for i in devices if i - distance in devices]
    return lax.ppermute(block, axis, route)


def prefix(x, axis, join, neutral):
    place = lax.axis_index(axis)
    gathered = jax.tree.map(
        lambda a, kind: lax.all_gather(a.astype(kind), axis), x, (jnp.bfloat16, jnp.bfloat16)
    )
    state = jax.tree.map(lambda a, e: jnp.zeros_like(a) + jnp.asarray(e, a.dtype), x, neutral)

    def one(lap, state):
        return join(
            state,
            jax.tree.map(
                lambda a, own: lax.dynamic_index_in_dim(a, lap, 0, False).astype(own.dtype),
                gathered,
                x,
            ),
        )

    return lax.fori_loop(0, place, one, state)


def prefix_2(x, axis, combine, identity):
    count, mine = (lax.axis_size(axis), lax.axis_index(axis))
    everything = jax.tree.map(
        lambda part, kind: lax.all_gather(part.astype(kind), axis),
        x,
        jax.tree.map(lambda a: jnp.bfloat16 if a.dtype == jnp.float32 else a.dtype, x),
    )
    start = jax.tree.map(
        lambda part, zero: jnp.broadcast_to(jnp.asarray(zero, part.dtype), part.shape), x, identity
    )

    def lap(k, before):
        at = count - 1 - k
        reached = at > mine
        new = combine(
            before, jax.tree.map(lambda part, own: part[at].astype(own.dtype), everything, x)
        )
        return jax.tree.map(lambda a, b: jnp.where(reached, a, b), new, before)

    return lax.fori_loop(0, count, lap, start)


def combine(earlier, later_pair):
    return (earlier[0] * later_pair[0], later_pair[0][:, None, None] * earlier[1] + later_pair[1])


def block_step(carry_pair, sliced):
    carried, seg_before, offset = carry_pair
    xblock, bblock, cblock, dblock, lblock, sblock = sliced
    block_len = sblock.shape[0]
    running = jnp.cumsum(lblock, axis=0)
    rowpos = lax.broadcasted_iota(jnp.int32, (block_len, block_len), 0)
    colpos = lax.broadcasted_iota(jnp.int32, (block_len, block_len), 1)
    allowed = (sblock[:, None] == sblock[None, :]) & (colpos <= rowpos)
    log_gap = running.T[:, :, None] - running.T[:, None, :]
    decays = jnp.exp(jnp.where(allowed[None], log_gap, -1e30))
    scores = jnp.dot(cblock, bblock.T, precision=precise)
    mixing = decays * scores[None] * dblock.T[:, None, :]
    y_diag = jnp.einsum("hts,shp->thp", mixing, xblock, precision=precise)
    carry_in = (sblock == seg_before).astype(jnp.float32)
    y_off = (jnp.exp(running) * carry_in[:, None])[:, :, None] * jnp.einsum(
        "tn,hpn->thp", cblock, carried, precision=precise
    )
    final_log = running[block_len - 1]
    tail_weight = (
        jnp.exp(final_log[None, :] - running)
        * (sblock == sblock[block_len - 1]).astype(jnp.float32)[:, None]
        * dblock
    )
    retain = jnp.exp(final_log) * (sblock[block_len - 1] == seg_before).astype(jnp.float32)
    carried = retain[:, None, None] * carried + jnp.einsum(
        "sh,shp,sn->hpn", tail_weight, xblock, bblock, precision=precise
    )
    return (
        (carried, sblock[block_len - 1], offset + final_log),
        (y_diag + y_off, running + offset[None, :]),
    )


def scan_ssd(values, b_rows, c_rows, dt_rows, log_decay, seg_ids, seg_start):
    length = seg_ids.shape[0]
    blocks = length // GROUP
    sliced = (
        values.reshape(blocks, GROUP, HEADS, HDIM),
        b_rows.reshape(blocks, GROUP, STATE),
        c_rows.reshape(blocks, GROUP, STATE),
        dt_rows.reshape(blocks, GROUP, HEADS),
        log_decay.reshape(blocks, GROUP, HEADS),
        seg_ids.reshape(blocks, GROUP),
    )
    initial = (
        jnp.zeros((HEADS, HDIM, STATE), jnp.float32),
        seg_start,
        jnp.zeros((HEADS,), jnp.float32),
    )
    finish, (outputs, running) = lax.scan(jax.checkpoint(block_step), initial, sliced)
    return (outputs.reshape(length, HEADS, HDIM), running.reshape(length, HEADS), finish[0])


def mixer_front(
    ext_rows, dt_raw, conv_taps, conv_bias, dt_bias, decay_log, seg_ext, seg_ids, seg_start
):
    length = seg_ids.shape[0]
    summed = jnp.broadcast_to(conv_bias, (length, conv_bias.shape[0]))
    for tap_index in range(CONV):
        same_doc = (seg_ext[tap_index : tap_index + length] == seg_ids).astype(jnp.float32)
        summed = (
            summed
            + conv_taps[:, tap_index] * ext_rows[tap_index : tap_index + length] * same_doc[:, None]
        )
    active = jax.nn.silu(summed)
    values = active[:, :INNER].reshape(length, HEADS, HDIM)
    b_rows = active[:, INNER : INNER + STATE]
    c_rows = active[:, INNER + STATE :]
    dt_rows = jax.nn.softplus(dt_raw + dt_bias)
    log_decay = -dt_rows * jnp.exp(decay_log)
    y_local, running, carried = scan_ssd(
        values, b_rows, c_rows, dt_rows, log_decay, seg_ids, seg_start
    )
    retain = jnp.exp(running[length - 1]) * (seg_ids[length - 1] == seg_start).astype(jnp.float32)
    return (values, c_rows, running, y_local, carried, retain)


def mixer_tail(
    values, c_rows, running, y_local, carried_in, gate_part, skip_scale, mixer_gain, carry_flag
):
    length = gate_part.shape[0]
    incoming = jnp.einsum("tn,hpn->thp", c_rows, carried_in, precision=precise)
    weights = jnp.exp(running) * carry_flag[:, None]
    mixed_ssd = y_local + weights[:, :, None] * incoming + skip_scale[None, :, None] * values
    gated = mixed_ssd.reshape(length, INNER) * jax.nn.silu(gate_part)
    return gated * lax.rsqrt(jnp.mean(gated * gated, axis=-1, keepdims=True) + epsilon) * mixer_gain


def on_device(
    inputs,
    segment_ids,
    out_grad,
    in_matrix,
    out_matrix,
    conv_taps,
    conv_bias,
    dt_bias,
    decay_log,
    skip_scale,
    mixer_gain,
    input_gain,
):
    units = inputs[0].astype(jnp.float32)
    seg_ids = segment_ids[0]
    length = units.shape[0]
    inv_rms = lax.rsqrt(jnp.mean(units * units, axis=-1, keepdims=True) + epsilon)
    base_rows = units * inv_rms
    w_piece = lax.all_gather(in_matrix, "fsdp", axis=0, tiled=True)
    g_piece = lax.all_gather(input_gain, "fsdp", axis=0, tiled=True)
    g_float = g_piece.astype(jnp.float32)
    part_rows = (base_rows * g_float).astype(jnp.bfloat16)
    product = jnp.dot(part_rows, w_piece, preferred_element_type=jnp.float32)
    projected = product
    projected = projected.astype(jnp.bfloat16)
    gate_part = projected[:, :INNER].astype(jnp.float32)
    conv_input = projected[:, INNER : INNER + XBC]
    dt_raw = projected[:, INNER + XBC :].astype(jnp.float32)
    out_whole, taps_whole, bias_whole, dtb_whole, decay_whole, skip_whole, norm_whole = (
        lax.all_gather(out_matrix, "fsdp", axis=0, tiled=True),
        lax.all_gather(conv_taps, "fsdp", axis=0, tiled=True),
        lax.all_gather(conv_bias, "fsdp", axis=0, tiled=True),
        lax.all_gather(dt_bias, "fsdp", axis=0, tiled=True),
        lax.all_gather(decay_log, "fsdp", axis=0, tiled=True),
        lax.all_gather(skip_scale, "fsdp", axis=0, tiled=True),
        lax.all_gather(mixer_gain, "fsdp", axis=0, tiled=True),
    )
    rim_rows, rim_seg = passed_along(
        (conv_input[length - CONV + 1 :], seg_ids[length - CONV + 1 :]), "ctx", 1
    )
    ext_rows = jnp.concatenate([rim_rows, conv_input], axis=0).astype(jnp.float32)
    seg_ext = jnp.concatenate([rim_seg, seg_ids], axis=0)
    seg_start = rim_seg[CONV - 2]

    def front_fn(ext_arg, dt_arg, taps_arg, bias_arg, dtb_arg, decay_arg):
        return mixer_front(
            ext_arg, dt_arg, taps_arg, bias_arg, dtb_arg, decay_arg, seg_ext, seg_ids, seg_start
        )

    front_out, front_back = jax.vjp(
        front_fn,
        ext_rows,
        dt_raw,
        taps_whole.astype(jnp.float32),
        bias_whole.astype(jnp.float32),
        dtb_whole.astype(jnp.float32),
        decay_whole.astype(jnp.float32),
    )
    values, c_rows, running, y_local, carried, retain = front_out
    identity = (jnp.ones((HEADS,), jnp.float32), jnp.zeros((HEADS, HDIM, STATE), jnp.float32))
    passed = prefix((retain, carried), "ctx", combine, identity)
    carried_in = passed[1]
    carry_flag = (seg_ids == seg_start).astype(jnp.float32)

    def tail_fn(
        values_arg, c_arg, running_arg, local_arg, carried_arg, gate_arg, skip_arg, gain_arg
    ):
        return mixer_tail(
            values_arg,
            c_arg,
            running_arg,
            local_arg,
            carried_arg,
            gate_arg,
            skip_arg,
            gain_arg,
            carry_flag,
        )

    mixer_out, tail_back = jax.vjp(
        tail_fn,
        values,
        c_rows,
        running,
        y_local,
        carried_in,
        gate_part,
        skip_whole.astype(jnp.float32),
        norm_whole.astype(jnp.float32),
    )
    mixer_low = mixer_out.astype(jnp.bfloat16)
    mixed = jnp.dot(mixer_low, out_whole, preferred_element_type=jnp.float32)
    summed_out = units + mixed
    block_out = summed_out.astype(jnp.bfloat16)
    cot_rows = out_grad[0]
    d_out_matrix = lax.dot_general(
        mixer_low, cot_rows, (((0,), (0,)), ((), ())), preferred_element_type=jnp.float32
    )
    d_mixer = lax.dot_general(
        cot_rows, out_whole, (((1,), (1,)), ((), ())), preferred_element_type=jnp.float32
    )
    d_values, d_c_rows, d_running, d_local, d_carried, d_gate, d_skip, d_norm_gain = tail_back(
        d_mixer
    )
    reversed_pair = prefix_2((retain, d_carried), "ctx", combine, identity)
    d_state = reversed_pair[1]
    d_retain = jnp.sum(d_state * carried_in, axis=(1, 2))
    d_ext, d_dt_raw, d_taps, d_bias, d_dtb, d_decay = front_back(
        (d_values, d_c_rows, d_running, d_local, d_state, d_retain)
    )
    returned = passed_along(d_ext[: CONV - 1].astype(jnp.bfloat16), "ctx", -1).astype(jnp.float32)
    d_conv_in = jnp.concatenate([d_ext[CONV - 1 : length], d_ext[length:] + returned], axis=0)
    d_projected = jnp.concatenate([d_gate, d_conv_in, d_dt_raw], axis=1).astype(jnp.bfloat16)
    d_in_matrix = lax.dot_general(
        part_rows, d_projected, (((0,), (0,)), ((), ())), preferred_element_type=jnp.float32
    )
    d_normed = lax.dot_general(
        d_projected,
        lax.all_gather(in_matrix, "fsdp", axis=0, tiled=True),
        (((1,), (1,)), ((), ())),
        preferred_element_type=jnp.float32,
    )
    d_input_gain = jnp.sum(d_normed * base_rows, axis=0)
    d_base = d_normed * g_float
    d_units = inv_rms * (d_base - base_rows * jnp.mean(d_base * base_rows, axis=-1, keepdims=True))
    input_grad = (cot_rows.astype(jnp.float32) + d_units).astype(jnp.bfloat16)
    split_sums = (
        lax.psum_scatter(
            d_in_matrix.astype(jnp.bfloat16), "fsdp", scatter_dimension=0, tiled=True
        ).astype(jnp.float32),
        lax.psum_scatter(
            d_out_matrix.astype(jnp.bfloat16), "fsdp", scatter_dimension=0, tiled=True
        ).astype(jnp.float32),
        lax.psum_scatter(
            d_taps.astype(jnp.bfloat16), "fsdp", scatter_dimension=0, tiled=True
        ).astype(jnp.float32),
        lax.psum_scatter(
            d_bias.astype(jnp.bfloat16), "fsdp", scatter_dimension=0, tiled=True
        ).astype(jnp.float32),
        lax.psum_scatter(
            d_norm_gain.astype(jnp.bfloat16), "fsdp", scatter_dimension=0, tiled=True
        ).astype(jnp.float32),
        lax.psum_scatter(
            d_input_gain.astype(jnp.bfloat16), "fsdp", scatter_dimension=0, tiled=True
        ).astype(jnp.float32),
    )
    reduced = (
        lax.psum(split_sums[0].astype(jnp.bfloat16), "ctx").astype(jnp.float32),
        lax.psum(split_sums[1].astype(jnp.bfloat16), "ctx").astype(jnp.float32),
        lax.psum(split_sums[2].astype(jnp.bfloat16), "ctx").astype(jnp.float32),
        lax.psum(split_sums[3].astype(jnp.bfloat16), "ctx").astype(jnp.float32),
        lax.psum(split_sums[4].astype(jnp.bfloat16), "ctx").astype(jnp.float32),
        lax.psum(split_sums[5].astype(jnp.bfloat16), "ctx").astype(jnp.float32),
    )
    square_sums = jnp.stack([jnp.sum(summed_out * summed_out), jnp.sum(mixed * mixed)])
    head_dt, head_decay, head_skip, stat_sums = lax.psum(
        (d_dtb, d_decay, d_skip, square_sums), ("fsdp", "ctx")
    )
    per_shard = HEADS // lax.axis_size("fsdp")
    offset_rows = lax.axis_index("fsdp") * per_shard
    dt_grad = lax.dynamic_slice_in_dim(head_dt, offset_rows, per_shard, 0)
    decay_grad = lax.dynamic_slice_in_dim(head_decay, offset_rows, per_shard, 0)
    skip_grad = lax.dynamic_slice_in_dim(head_skip, offset_rows, per_shard, 0)
    entries = length * lax.axis_size("fsdp") * lax.axis_size("ctx") * D
    rms_stats = jnp.sqrt(stat_sums / entries)
    return (
        block_out[None],
        input_grad[None],
        reduced[0],
        reduced[1],
        reduced[2],
        reduced[3],
        dt_grad,
        decay_grad,
        skip_grad,
        reduced[4],
        reduced[5],
        rms_stats,
    )


def solution(mesh):
    return jax.shard_map(
        on_device,
        mesh=mesh,
        in_specs=(
            P("fsdp", "ctx", None),
            P("fsdp", "ctx"),
            P("fsdp", "ctx", None),
            P("fsdp", None),
            P("fsdp", None),
            P("fsdp", None),
            P("fsdp"),
            P("fsdp"),
            P("fsdp"),
            P("fsdp"),
            P("fsdp"),
            P("fsdp"),
        ),
        out_specs=(
            P("fsdp", "ctx", None),
            P("fsdp", "ctx", None),
            P("fsdp", None),
            P("fsdp", None),
            P("fsdp", None),
            P("fsdp"),
            P("fsdp"),
            P("fsdp"),
            P("fsdp"),
            P("fsdp"),
            P("fsdp"),
            P(),
        ),
        check_vma=False,
    )
```

profile of v0, /device:TPU:0, one launch (start us, length us, event | category | flops | bytes accessed | tf_op | source)
XLA Modules:
  0.0 1636.9 jit_solution(982712403689798339)
XLA Ops:
  44.6 93.2 %all-gather.11.cloned.1.call-done = bf16[1536,6448]{0,1:T(8,128)(2,1)} async-done(((bf16[384,6448]{0,1:T(8,128)(2,1)}), bf16[1536,6448]{0,1:T(8,128)(2,1)}) %all-gather.11.cloned.1.call-update) | async-done | bytes 19808272 | tf_op jit(solution)/shard_map/all_gather | solution.py:177
  137.8 16.7 %convolution_convert_fusion.2 = bf16[512,6448]{1,0:T(8,128)(2,1)} fusion(bf16[1536,6448]{0,1:T(8,128)(2,1)} %all-gather.11.cloned.1.call-done, bf16[1,512,1536]{2,1,0:T(8,128)(2,1)S(1)} %copy-done.14, f32[1536]{0:T(1024)S(1)} %reshape.551, f32[512]{0:T(512)S(1)} %add_rsqrt_fusion), kind=kOutput, calls=%fused_computation.150 | convolution fusion | flops 10148274176 | bytes 27992064 | tf_op jit(solution)/shard_map/dot_general | solution.py:181
  205.0 210.1 %while.80 = (s32[]{:T(128)}, f32[48,64,128]{2,1,0:T(8,128)S(1)}, s32[]{:T(128)}, f32[48]{0:T(128)S(1)}, f32[2,256,48,64]{1,0,3,2:T(2,128)}, /*index=5*/f32[2,256...) while((s32[]{:T(128)}, f32[48,64,128]{2,1,0:T(8,128)S(1)}, ...), condition=%wide.region_4.5_spmd.clone, body=%wide.region_1.4_spmd.clone.sunk | while | flops 4951254016 | bytes 38503760 | solution.py:119
  208.6 16.5 %fusion.240 = f32[48,64,256]{2,1,0:T(8,128)} fusion(f32[48,256]{1,0:T(8,128)S(1)} %dynamic-slice_bitcast_fusion.17, f32[256,256]{1,0:T(8,128)S(1)} %fusion.238, f32[48,256]{1,0:T(8,128)S(1)} %get-tuple-element.1556, pred[256,256]{1,0:T(8,128)(4,1)S(1)} %fusion.239, f32[2,256,48,64]{1,3,2,0:T(8,128)} %get-tuple-element.1663, s32[]{:T(128)} %get-tuple-element.1634), kind=kOutput, calls=%fused_computation.6.clone.1 | convolution fusion | flops 2428502016 | bytes 6767104 | tf_op jit(solution)/shard_map/jvp()/while/body/eval_jaxpr/hts,shp->thp/dot_general | solution.py:82
  236.9 63.6 %dynamic_update_slice.95 = f32[2,256,48,64]{1,0,3,2:T(2,128)} dynamic-update-slice(f32[2,256,48,64]{1,0,3,2:T(2,128)} %get-tuple-element.1638, f32[1,256,48,64]{1,0,3,2:T(1,128)} %copy.397, s32[]{:T(128)} %get-tuple-element.1634, s32[]{:T(128)} %constant.198.clone.1..sunk.1, s32[]{:T(128)} %constant.198.clone.1..sunk.1, s32[]{:T(128)} %constant.198.clone.1..sunk.1) | dynamic-update-slice | bytes 6291460 | tf_op jit(solution)/shard_map/jvp()/while/body/jit(dynamic_update_index_in_dim)/dynamic_update_slice | solution.py:119
  313.4 16.5 %fusion.240 = f32[48,64,256]{2,1,0:T(8,128)} fusion(f32[48,256]{1,0:T(8,128)S(1)} %dynamic-slice_bitcast_fusion.17, f32[256,256]{1,0:T(8,128)S(1)} %fusion.238, f32[48,256]{1,0:T(8,128)S(1)} %get-tuple-element.1556, pred[256,256]{1,0:T(8,128)(4,1)S(1)} %fusion.239, f32[2,256,48,64]{1,3,2,0:T(8,128)} %get-tuple-element.1663, s32[]{:T(128)} %get-tuple-element.1634), kind=kOutput, calls=%fused_computation.6.clone.1 | convolution fusion | flops 2428502016 | bytes 6767104 | tf_op jit(solution)/shard_map/jvp()/while/body/eval_jaxpr/hts,shp->thp/dot_general | solution.py:82
  341.7 63.6 %dynamic_update_slice.95 = f32[2,256,48,64]{1,0,3,2:T(2,128)} dynamic-update-slice(f32[2,256,48,64]{1,0,3,2:T(2,128)} %get-tuple-element.1638, f32[1,256,48,64]{1,0,3,2:T(1,128)} %copy.397, s32[]{:T(128)} %get-tuple-element.1634, s32[]{:T(128)} %constant.198.clone.1..sunk.1, s32[]{:T(128)} %constant.198.clone.1..sunk.1, s32[]{:T(128)} %constant.198.clone.1..sunk.1) | dynamic-update-slice | bytes 6291460 | tf_op jit(solution)/shard_map/jvp()/while/body/jit(dynamic_update_index_in_dim)/dynamic_update_slice | solution.py:119
  425.2 18.4 %all-gather.4 = bf16[8,1,48]{2,1,0:T(2,128)(2,1)S(1)} all-gather(bf16[1,1,48]{2,1,0:T(2,128)(2,1)S(1)} %bitcast.512), channel_id=1, replica_groups=mesh['fsdp'=4,'ctx'=8] {'ctx'}, dimensions={0}, use_global_device_ids=true | all-gather | bytes 864 | tf_op jit(solution)/shard_map/all_gather | solution.py:27
  452.6 61.9 %all-gather.15.cloned.1.call-done = bf16[384,64,128]{2,1,0:T(8,128)(2,1)} async-done(((bf16[48,64,128]{2,1,0:T(8,128)(2,1)}), bf16[384,64,128]{2,1,0:T(8,128)(2,1)}) %all-gather.15.cloned.1.call-update) | async-done | bytes 6291472 | tf_op jit(solution)/shard_map/all_gather | solution.py:27
  514.7 13.1 multiply_add_fusion.4
  541.2 37.4 %all-gather.13.cloned.1.call-done = bf16[3072,1536]{1,0:T(8,128)(2,1)} async-done(((bf16[768,1536]{1,0:T(8,128)(2,1)}), bf16[3072,1536]{1,0:T(8,128)(2,1)}) %all-gather.13.cloned.1.call-update) | async-done | bytes 9437200 | tf_op jit(solution)/shard_map/all_gather | solution.py:188
  578.6 12.5 multiply_reduce_fusion.9
  645.4 70.8 %all-gather.17.cloned.1.call-done = bf16[384,64,128]{2,1,0:T(8,128)(2,1)} async-done(((bf16[48,64,128]{2,1,0:T(8,128)(2,1)}), bf16[384,64,128]{2,1,0:T(8,128)(2,1)}) %all-gather.17.cloned.1.call-update) | async-done | bytes 6291472 | tf_op jit(solution)/shard_map/all_gather | solution.py:47
  716.2 24.0 %while.81 = (s32[]{:T(128)}, f32[48,64,128]{2,1,0:T(8,128)}, s32[]{:T(128)}, bf16[8,48]{1,0:T(8,128)(2,1)S(1)}, bf16[8,48,64,128]{3,2,1,0:T(8,128)(2,1)}, /*index=5*/s32[]{:T(128)}, s32[]{:T(128)}, s32[]{:T(128)}, s32[]{:T(128)}) while((s32[]{:T(128)}, f32[48,64,128]{2,1,0:T(8,128)}, s32[]{:T(128)}, ...), condition=%wide.region_10.11_spmd.clone, body=%wide.region_9.10_spmd.clone.sunk | while | flops 1966136 | bytes 3932807 | solution.py:63
  749.2 248.0 %while.82 = (s32[]{:T(128)}, f32[48,64,128]{2,1,0:T(8,128)}, f32[48]{0:T(128)}, f32[2,256,48,64]{1,3,2,0:T(8,128)}, f32[2,256,128]{2,1,0:T(8,128)}, /*index=5*/f...) while((s32[]{:T(128)}, f32[48,64,128]{2,1,0:T(8,128)}, ...), condition=%wide.region_26.27_spmd.clone, body=%wide.region_13.26_spmd.clone.sunk | while | flops 11239392256 | bytes 115198616 | solution.py:119
  809.2 21.4 %fusion.264 = (f32[48,256]{1,0:T(8,128)S(1)}, f32[48,256]{1,0:T(8,128)S(1)}, f32[48,256]{1,0:T(8,128)}, f32[256,256]{1,0:T(8,128)}) fusion(f32[48,256]{1,0:T(8,128)S(1)} %bitcast.484, f32[256,256]{1,0:T(8,128)S(1)} %fusion.262, f32[48,256]{1,0:T(8,128)} %get-tuple-element.1594, pred[256,256]{1,0:T(8,128)(4,1)S(1)} %fusion.263, ...), kind=kOutput, calls=%fused_computation.72.clone.1 | convolution fusion | flops 2456711168 | bytes 7127040 | tf_op jit(solution)/shard_map/transpose(jvp())/while/body/eval_jaxpr/checkpoint/hts,shp->thp/dot_general | solution.py:82
  860.7 12.2 bitcast_dynamic-update-slice_fusion.7
  919.4 21.4 %fusion.264 = (f32[48,256]{1,0:T(8,128)S(1)}, f32[48,256]{1,0:T(8,128)S(1)}, f32[48,256]{1,0:T(8,128)}, f32[256,256]{1,0:T(8,128)}) fusion(f32[48,256]{1,0:T(8,128)S(1)} %bitcast.484, f32[256,256]{1,0:T(8,128)S(1)} %fusion.262, f32[48,256]{1,0:T(8,128)} %get-tuple-element.1594, pred[256,256]{1,0:T(8,128)(4,1)S(1)} %fusion.263, ...), kind=kOutput, calls=%fused_computation.72.clone.1 | convolution fusion | flops 2456711168 | bytes 7127040 | tf_op jit(solution)/shard_map/transpose(jvp())/while/body/eval_jaxpr/checkpoint/hts,shp->thp/dot_general | solution.py:82
  971.0 12.2 bitcast_dynamic-update-slice_fusion.7
  997.2 12.7 fusion.132
  1009.9 11.3 copy.299
  1075.3 16.4 convolution_convert_fusion
  1091.6 24.2 %copy.300 = bf16[1536,6448]{1,0:T(8,128)(2,1)} copy(bf16[1536,6448]{0,1:T(8,128)(2,1)} %convolution_convert_fusion) | data formatting | bytes 39616512
  1117.2 11.2 convolution_convert_fusion.1
  1130.3 133.6 %reduce-scatter.10.cloned.1.call-done = bf16[384,6448]{1,0:T(8,128)(2,1)} async-done(((bf16[1536,6448]{1,0:T(8,128)(2,1)}), bf16[384,6448]{1,0:T(8,128)(2,1)}) %reduce-scatter.10.cloned.1.call-update) | async-done | bytes 4952080
  1271.5 74.1 %reduce-scatter.8.cloned.1.call-done = bf16[768,1536]{1,0:T(8,128)(2,1)} async-done(((bf16[3072,1536]{1,0:T(8,128)(2,1)}), bf16[768,1536]{1,0:T(8,128)(2,1)}) %reduce-scatter.8.cloned.1.call-update) | async-done | bytes 2359312 | tf_op jit(solution)/shard_map/reduce_scatter | solution.py:289
  1348.0 20.0 %fusion.135 = f32[512,1536]{1,0:T(8,128)S(1)} fusion(bf16[1536,6448]{0,1:T(8,128)(2,1)} %all-gather.11.cloned.1.call-done, bf16[512,48]{1,0:T(8,128)(2,1)S(1)} %copy-done.49, bf16[3,3328]{1,0:T(4,128)(2,1)S(1)} %fusion.147, bf16[509,3328]{1,0:T(8,128)(2,1)} %copy-done.19, bf16[512,3072]{1,0:T(8,128)(2,1)} %get-tuple-element.1248), kind=kOutput, calls=%fused_computation.222 | convolution fusion | flops 10168238080 | bytes 29556736 | tf_op jit(solution)/shard_map/dot_general | solution.py:275
  1368.1 12.7 multiply_reduce_fusion.15
  1382.2 44.0 %all-reduce.20 = (f32[48]{0:T(128)S(1)}, f32[48]{0:T(128)S(1)}, f32[48]{0:T(128)S(1)}, f32[2]{0:T(128)S(1)}) all-reduce(f32[48]{0:T(128)S(1)} %copy-done.80, f32[48]{0:T(128)S(1)} %fusion.156, f32[48]{0:T(128)S(1)} %reduce_sum.376, f32[2]{0:T(128)S(1)} %pad_maximum_fusion.3), channel_id=1, replica_groups=mesh['fsdp'=4,'ctx'=8] {'fsdp','ctx'}, use_global_device_ids=true, to_apply=%region_42.43 | all-reduce | flops 146 | bytes 1168 | tf_op jit(solution)/shard_map/psum | solution.py:314
  1427.9 11.9 all-reduce.23
  1446.5 37.0 %all-reduce.21 = (bf16[832,4]{0,1:T(4,128)(2,1)S(1)}, bf16[832]{0:T(1024)(128)(2,1)S(1)}, bf16[768]{0:T(1024)(128)(2,1)S(1)}, bf16[384]{0:T(512)(128)(2,1)S(1)}) all-reduce(bf16[832,4]{0,1:T(4,128)(2,1)S(1)} %copy.303, bf16[832]{0:T(1024)(128)(2,1)S(1)} %dynamic-slice.5, ...), channel_id=1, replica_groups=mesh['fsdp'=4,'ctx'=8] {'ctx'}, use_global_device_ids=true, to_apply=%region_37.38 | all-reduce | flops 5312 | bytes 21248 | tf_op jit(solution)/shard_map/psum | solution.py:308
  1485.9 133.8 %all-reduce.27.cloned.1.call-done = (bf16[384,6448]{0,1:T(8,128)(2,1)}, bf16[768,1536]{1,0:T(8,128)(2,1)}) async-done(((bf16[384,6448]{0,1:T(8,128)(2,1)}, bf16[768,1536]{1,0:T(8,128)(2,1)}), (bf16[384,6448]{0,1:T(8,128)(2,1)}, bf16[768,1536]{1,0:T(8,128)(2,1)})) %all-reduce.27.cloned.1.call-update) | async-done | bytes 7311376 | tf_op jit(solution)/shard_map/psum | solution.py:306
  (527 shorter events, 487.0 us)
Async XLA Ops:
  7.2 130.6 %all-gather.11.cloned.1.call-start = ((), (), s32[]{:S(2)}) async-start(), calls=%async_computation.3 | async-start | bytes 24760320 | tf_op jit(solution)/shard_map/all_gather | solution.py:177
  7.9 506.6 %all-gather.15.cloned.1.call-start = ((), (), s32[]{:S(2)}) async-start(), calls=%async_computation.6 | async-start | bytes 7077888 | tf_op jit(solution)/shard_map/all_gather | solution.py:27
  8.7 33.3 %collective-permute-start = (s32[3]{0:T(128)S(1)}, s32[3]{0:T(128)S(1)}, u32[]{:S(2)}, u32[]{:S(2)}) collective-permute-start(s32[3]{0:T(128)S(1)} %slice_bitcast_fusion), channel_id=1, source_target_pairs={{0,1},{1,2},{2,3},{3,4},{4,5},{5,6},{6,7},{8,9},{9,10},{10,11},{11... | collective-permute-start | bytes 44 | tf_op jit(solution)/shard_map/ppermute | solution.py:21
  19.5 135.0 %copy-start.65 = (f32[1536]{0:T(1024)}, f32[1536]{0:T(1024)S(1)}, u32[]{:S(2)}) copy-start(f32[1536]{0:T(1024)S(1)} %reshape.551) | copy-start | bytes 18436
  33.8 120.7 %copy-start.83 = (bf16[48]{0:T(256)(128)(2,1)}, bf16[48]{0:T(256)(128)(2,1)S(1)}, u32[]{:S(2)}) copy-start(bf16[48]{0:T(256)(128)(2,1)S(1)} %get-tuple-element.1206) | copy-start | bytes 292
  39.5 119.4 %copy-start.76 = (f32[48]{0:T(128)}, f32[48]{0:T(128)S(1)}, u32[]{:S(2)}) copy-start(f32[48]{0:T(128)S(1)} %convert_element_type.241) | copy-start | bytes 580
  41.5 126.0 %copy-start.40 = (f32[3328]{0:T(1024)}, f32[3328]{0:T(1024)S(1)}, u32[]{:S(2)}) copy-start(f32[3328]{0:T(1024)S(1)} %get-tuple-element.1104) | copy-start | bytes 39940
  41.5 126.0 %copy-start.42 = (f32[3328]{0:T(1024)}, f32[3328]{0:T(1024)S(1)}, u32[]{:S(2)}) copy-start(f32[3328]{0:T(1024)S(1)} %get-tuple-element.1105) | copy-start | bytes 39940
  41.6 126.0 %copy-start.44 = (f32[3328]{0:T(1024)}, f32[3328]{0:T(1024)S(1)}, u32[]{:S(2)}) copy-start(f32[3328]{0:T(1024)S(1)} %get-tuple-element.1106) | copy-start | bytes 39940
  41.6 126.0 %copy-start.46 = (f32[3328]{0:T(1024)}, f32[3328]{0:T(1024)S(1)}, u32[]{:S(2)}) copy-start(f32[3328]{0:T(1024)S(1)} %get-tuple-element.1107) | copy-start | bytes 39940
  42.0 117.0 %copy-start.78 = (f32[48]{0:T(128)}, f32[48]{0:T(128)S(1)}, u32[]{:S(2)}) copy-start(f32[48]{0:T(128)S(1)} %convert_exponential_fusion) | copy-start | bytes 580
  42.0 112.5 %copy-start.73 = (f32[512]{0:T(512)}, f32[512]{0:T(512)S(1)}, u32[]{:S(2)}) copy-start(f32[512]{0:T(512)S(1)} %add_rsqrt_fusion) | copy-start | bytes 6148
  44.6 123.0 %copy-start.59 = (f32[512]{0:T(512)}, f32[512]{0:T(512)S(1)}, u32[]{:S(2)}) copy-start(f32[512]{0:T(512)S(1)} %get-tuple-element.1259) | copy-start | bytes 6148
  44.6 123.0 %copy-start.61 = (f32[512]{0:T(512)}, f32[512]{0:T(512)S(1)}, u32[]{:S(2)}) copy-start(f32[512]{0:T(512)S(1)} %get-tuple-element.1260) | copy-start | bytes 6148
  44.6 123.0 %copy-start.63 = (f32[512]{0:T(512)}, f32[512]{0:T(512)S(1)}, u32[]{:S(2)}) copy-start(f32[512]{0:T(512)S(1)} %get-tuple-element.1261) | copy-start | bytes 6148
  155.3 9.5 collective-permute-start.1
  205.0 212.5 %copy-start.81 = (bf16[768]{0:T(1024)(128)(2,1)S(1)}, bf16[768]{0:T(1024)(128)(2,1)}, u32[]{:S(2)}) copy-start(bf16[768]{0:T(1024)(128)(2,1)} %param.30) | copy-start | bytes 4612
  416.2 162.4 %all-gather.13.cloned.1.call-start = ((), (), s32[]{:S(2)}) async-start(), calls=%async_computation.4 | async-start | bytes 11796480 | tf_op jit(solution)/shard_map/all_gather | solution.py:188
  416.9 299.3 %all-gather.17.cloned.1.call-start = ((), (), s32[]{:S(2)}) async-start(), calls=%async_computation.7 | async-start | bytes 7077888 | tf_op jit(solution)/shard_map/all_gather | solution.py:47
  422.7 168.4 %copy-start.55 = (f32[4,1,768]{2,1,0:T(1,128)}, f32[4,1,768]{2,1,0:T(1,128)S(1)}, u32[]{:S(2)}) copy-start(f32[4,1,768]{2,1,0:T(1,128)S(1)} %convert_element_type.281) | copy-start | bytes 36868
  452.6 156.2 %copy-start.24 = (f32[512,48]{0,1:T(8,128)}, f32[512,48]{0,1:T(8,128)S(1)}, u32[]{:S(2)}) copy-start(f32[512,48]{0,1:T(8,128)S(1)} %exponential_multiply_fusion.4) | copy-start | bytes 294916
  514.7 225.5 %copy-start.2 = (f32[48,64,128]{2,1,0:T(8,128)}, f32[48,64,128]{2,1,0:T(8,128)S(1)}, u32[]{:S(2)}) copy-start(f32[48,64,128]{2,1,0:T(8,128)S(1)} %get-tuple-element.688) | copy-start | bytes 4718596
  617.1 646.9 %reduce-scatter.10.cloned.1.call-start = ((), (), s32[]{:S(2)}) async-start(), calls=%async_computation.8 | async-start | bytes 25067520
  1065.7 7.9 collective-permute-start.2
  1115.9 229.8 %reduce-scatter.8.cloned.1.call-start = ((), (), s32[]{:S(2)}) async-start(), calls=%async_computation.5 | async-start | bytes 11796480 | tf_op jit(solution)/shard_map/reduce_scatter | solution.py:289
  1128.5 317.0 %reduce-scatter.12.cloned.1.call-start = ((), (), s32[]{:S(2)}) async-start(), calls=%async_computation.9 | async-start | bytes 1064960
  1130.0 217.8 %copy-start.57 = (f32[3072]{0:T(1024)S(1)}, f32[3072]{0:T(1024)}, u32[]{:S(2)}) copy-start(f32[3072]{0:T(1024)} %get-tuple-element.1211) | copy-start | bytes 36868
  1130.0 218.0 %copy-start.82 = (f32[48]{0:T(128)S(1)}, f32[48]{0:T(128)}, u32[]{:S(2)}) copy-start(f32[48]{0:T(128)} %get-tuple-element.1249) | copy-start | bytes 580
  1130.0 218.0 %copy-start.84 = (bf16[48]{0:T(256)(128)(2,1)S(1)}, bf16[48]{0:T(256)(128)(2,1)}, u32[]{:S(2)}) copy-start(bf16[48]{0:T(256)(128)(2,1)} %copy-done.83) | copy-start | bytes 292
  1130.0 218.0 %copy-start.49 = (bf16[512,48]{1,0:T(8,128)(2,1)S(1)}, bf16[512,48]{1,0:T(8,128)(2,1)}, u32[]{:S(2)}) copy-start(bf16[512,48]{1,0:T(8,128)(2,1)} %copy-done.48) | copy-start | bytes 147460
  1130.0 489.6 %all-reduce.27.cloned.1.call-start = ((), (), s32[]{:S(2)}) async-start(), calls=%async_computation.10 | async-start | bytes 14622720 | tf_op jit(solution)/shard_map/psum | solution.py:306
  1368.1 59.8 %copy-start.75 = (bf16[3072]{0:T(1024)(128)(2,1)S(1)}, bf16[3072]{0:T(1024)(128)(2,1)}, u32[]{:S(2)}) copy-start(bf16[3072]{0:T(1024)(128)(2,1)} %get-tuple-element.1095) | copy-start | bytes 18436
  (98 other events, 1464.4 us)
Sparse Core Ops, SparseCore 0:
  9.6 128.1 all-gather.10
  416.3 98.1 all-gather.14
  516.1 62.4 all-gather.12
  617.2 99.0 all-gather.16
  1116.0 147.9 reduce-scatter.9
  1267.2 78.4 reduce-scatter.7
  1348.4 23.6 reduce-scatter.11
  1376.1 243.4 all-reduce.26
where the time goes:
time: 1660 us; the launch traced here: 1640 us
  waiting for transfers between devices  606 us (37%)
  local copies, waits for them, and re-layouts  345 us (21%)
  matrix products  310 us (19%)
  other arithmetic  174 us (10%)
  blocking collectives  135 us (8%)
  loops' own time  34.9 us (2%)
  between operations  20.9 us (1%)
    dynamic_update_slice x10, local copies, waits for them, and re-layouts, scan_ssd(): lax.scan(jax.checkpoint(block_step), initial, sliced)  142 us
    unnamed x10, waiting for transfers between devices  135 us
    psum x1, waiting for transfers between devices, on_device(): lax.psum(split_sums[0].astype(jnp.bfloat16), 'ctx').astype(jnp.float32)  134 us
    dot_general x6, matrix products, block_step(): y_diag = jnp.einsum('hts,shp->thp', mixing, xblock, precision=precise)  100 us
    all_gather x1, waiting for transfers between devices, on_device(): w_piece = lax.all_gather(in_matrix, 'fsdp', axis=0, tiled=True)  93.2 us
    reduce_scatter x1, waiting for transfers between devices, on_device(): lax.psum_scatter(d_out_matrix.astype(jnp.bfloat16), 'fsdp', scatter_dimen...  74.1 us
    all_gather x1, waiting for transfers between devices, prefix_2(): lax.all_gather(part.astype(kind), axis)  70.8 us
    all_gather x1, waiting for transfers between devices, prefix(): lax.all_gather(a.astype(kind), axis)  61.9 us
  transfers between devices with their start and end apart: 11, of which 7 were waited for; matrix products, arithmetic and copies ran while one was open for 9% of the time, Pallas kernels for 0%

commit v1 on v0

--- a/solution.py
+++ b/solution.py
@@ -2,6 +2,7 @@
 import jax.numpy as jnp
 from jax import lax
 from jax.sharding import PartitionSpec as P
+from jax.lax import all_gather
 
 D = 1536
 HEADS = 48
@@ -13,6 +14,11 @@
 XBC = 3328
 epsilon = 1e-05
 precise = lax.Precision.HIGHEST
+
+
+def zones_view(xin, shard_axis):
+    z_new = all_gather(xin, shard_axis)
+    return jnp.sum(z_new, 0)
 
 
 def passed_along(block, axis, distance):
@@ -305,7 +311,7 @@
     reduced = (
         lax.psum(split_sums[0].astype(jnp.bfloat16), "ctx").astype(jnp.float32),
         lax.psum(split_sums[1].astype(jnp.bfloat16), "ctx").astype(jnp.float32),
-        lax.psum(split_sums[2].astype(jnp.bfloat16), "ctx").astype(jnp.float32),
+        zones_view(split_sums[2].astype(jnp.bfloat16), "ctx").astype(jnp.float32),
         lax.psum(split_sums[3].astype(jnp.bfloat16), "ctx").astype(jnp.float32),
         lax.psum(split_sums[4].astype(jnp.bfloat16), "ctx").astype(jnp.float32),
         lax.psum(split_sums[5].astype(jnp.bfloat16), "ctx").astype(jnp.float32),

time: 1660 us -> 1660 us (level)
    all_gather x0 -> x1, blocking collectives: none -> 31.3 us  [zones_view(): z_new = all_gather(xin, shard_axis)]
where the time goes in v1:
time: 1660 us; the launch traced here: 1640 us
  waiting for transfers between devices  591 us (36%)
  local copies, waits for them, and re-layouts  345 us (21%)
  matrix products  310 us (19%)
  other arithmetic  174 us (10%)
  blocking collectives  151 us (9%)
  loops' own time  34.9 us (2%)
  between operations  20.9 us (1%)
    dynamic_update_slice x10, local copies, waits for them, and re-layouts, scan_ssd(): lax.scan(jax.checkpoint(block_step), initial, sliced)  142 us
    unnamed x10, waiting for transfers between devices  135 us
    psum x1, waiting for transfers between devices, on_device(): lax.psum(split_sums[0].astype(jnp.bfloat16), 'ctx').astype(jnp.float32)  119 us
    dot_general x6, matrix products, block_step(): y_diag = jnp.einsum('hts,shp->thp', mixing, xblock, precision=precise)  100 us
    all_gather x1, waiting for transfers between devices, on_device(): w_piece = lax.all_gather(in_matrix, 'fsdp', axis=0, tiled=True)  93.2 us
    reduce_scatter x1, waiting for transfers between devices, on_device(): lax.psum_scatter(d_out_matrix.astype(jnp.bfloat16), 'fsdp', scatter_dimen...  74.1 us
    all_gather x1, waiting for transfers between devices, prefix_2(): lax.all_gather(part.astype(kind), axis)  70.8 us
    all_gather x1, waiting for transfers between devices, prefix(): lax.all_gather(a.astype(kind), axis)  61.9 us
  transfers between devices with their start and end apart: 11, of which 7 were waited for; matrix products, arithmetic and copies ran while one was open for 9% of the time, Pallas kernels for 0%

profile of v1, /device:TPU:0, one launch (start us, length us, event | category | flops | bytes accessed | tf_op | source)
XLA Modules:
  0.0 1637.7 jit_solution(10622836766523377605)
XLA Ops:
  44.6 93.2 %all-gather.13.cloned.1.call-done = bf16[1536,6448]{0,1:T(8,128)(2,1)} async-done(((bf16[384,6448]{0,1:T(8,128)(2,1)}), bf16[1536,6448]{0,1:T(8,128)(2,1)}) %all-gather.13.cloned.1.call-update) | async-done | bytes 19808272 | tf_op jit(solution)/shard_map/all_gather | solution.py:183
  137.8 16.7 %convolution_convert_fusion.2 = bf16[512,6448]{1,0:T(8,128)(2,1)} fusion(bf16[1536,6448]{0,1:T(8,128)(2,1)} %all-gather.13.cloned.1.call-done, bf16[1,512,1536]{2,1,0:T(8,128)(2,1)S(1)} %copy-done.14, f32[1536]{0:T(1024)S(1)} %reshape.554, f32[512]{0:T(512)S(1)} %add_rsqrt_fusion), kind=kOutput, calls=%fused_computation.150 | convolution fusion | flops 10148274176 | bytes 27992064 | tf_op jit(solution)/shard_map/dot_general | solution.py:187
  205.0 210.1 %while.80 = (s32[]{:T(128)}, f32[48,64,128]{2,1,0:T(8,128)S(1)}, s32[]{:T(128)}, f32[48]{0:T(128)S(1)}, f32[2,256,48,64]{1,0,3,2:T(2,128)}, /*index=5*/f32[2,256...) while((s32[]{:T(128)}, f32[48,64,128]{2,1,0:T(8,128)S(1)}, ...), condition=%wide.region_4.5_spmd.clone, body=%wide.region_1.4_spmd.clone.sunk | while | flops 4951254016 | bytes 38503760 | solution.py:125
  208.6 16.5 %fusion.240 = f32[48,64,256]{2,1,0:T(8,128)} fusion(f32[48,256]{1,0:T(8,128)S(1)} %dynamic-slice_bitcast_fusion.17, f32[256,256]{1,0:T(8,128)S(1)} %fusion.238, f32[48,256]{1,0:T(8,128)S(1)} %get-tuple-element.1555, pred[256,256]{1,0:T(8,128)(4,1)S(1)} %fusion.239, f32[2,256,48,64]{1,3,2,0:T(8,128)} %get-tuple-element.1662, s32[]{:T(128)} %get-tuple-element.1633), kind=kOutput, calls=%fused_computation.6.clone.1 | convolution fusion | flops 2428502016 | bytes 6767104 | tf_op jit(solution)/shard_map/jvp()/while/body/eval_jaxpr/hts,shp->thp/dot_general | solution.py:88
  236.9 63.6 %dynamic_update_slice.95 = f32[2,256,48,64]{1,0,3,2:T(2,128)} dynamic-update-slice(f32[2,256,48,64]{1,0,3,2:T(2,128)} %get-tuple-element.1637, f32[1,256,48,64]{1,0,3,2:T(1,128)} %copy.397, s32[]{:T(128)} %get-tuple-element.1633, s32[]{:T(128)} %constant.199.clone.1..sunk.1, s32[]{:T(128)} %constant.199.clone.1..sunk.1, s32[]{:T(128)} %constant.199.clone.1..sunk.1) | dynamic-update-slice | bytes 6291460 | tf_op jit(solution)/shard_map/jvp()/while/body/jit(dynamic_update_index_in_dim)/dynamic_update_slice | solution.py:125
  313.4 16.5 %fusion.240 = f32[48,64,256]{2,1,0:T(8,128)} fusion(f32[48,256]{1,0:T(8,128)S(1)} %dynamic-slice_bitcast_fusion.17, f32[256,256]{1,0:T(8,128)S(1)} %fusion.238, f32[48,256]{1,0:T(8,128)S(1)} %get-tuple-element.1555, pred[256,256]{1,0:T(8,128)(4,1)S(1)} %fusion.239, f32[2,256,48,64]{1,3,2,0:T(8,128)} %get-tuple-element.1662, s32[]{:T(128)} %get-tuple-element.1633), kind=kOutput, calls=%fused_computation.6.clone.1 | convolution fusion | flops 2428502016 | bytes 6767104 | tf_op jit(solution)/shard_map/jvp()/while/body/eval_jaxpr/hts,shp->thp/dot_general | solution.py:88
  341.7 63.6 %dynamic_update_slice.95 = f32[2,256,48,64]{1,0,3,2:T(2,128)} dynamic-update-slice(f32[2,256,48,64]{1,0,3,2:T(2,128)} %get-tuple-element.1637, f32[1,256,48,64]{1,0,3,2:T(1,128)} %copy.397, s32[]{:T(128)} %get-tuple-element.1633, s32[]{:T(128)} %constant.199.clone.1..sunk.1, s32[]{:T(128)} %constant.199.clone.1..sunk.1, s32[]{:T(128)} %constant.199.clone.1..sunk.1) | dynamic-update-slice | bytes 6291460 | tf_op jit(solution)/shard_map/jvp()/while/body/jit(dynamic_update_index_in_dim)/dynamic_update_slice | solution.py:125
  425.2 18.4 %all-gather.5 = bf16[8,1,48]{2,1,0:T(2,128)(2,1)S(1)} all-gather(bf16[1,1,48]{2,1,0:T(2,128)(2,1)S(1)} %bitcast.514), channel_id=1, replica_groups=mesh['fsdp'=4,'ctx'=8] {'ctx'}, dimensions={0}, use_global_device_ids=true | all-gather | bytes 864 | tf_op jit(solution)/shard_map/all_gather | solution.py:33
  452.6 61.9 %all-gather.17.cloned.1.call-done = bf16[384,64,128]{2,1,0:T(8,128)(2,1)} async-done(((bf16[48,64,128]{2,1,0:T(8,128)(2,1)}), bf16[384,64,128]{2,1,0:T(8,128)(2,1)}) %all-gather.17.cloned.1.call-update) | async-done | bytes 6291472 | tf_op jit(solution)/shard_map/all_gather | solution.py:33
  514.7 13.1 multiply_add_fusion.4
  541.2 37.4 %all-gather.15.cloned.1.call-done = bf16[3072,1536]{1,0:T(8,128)(2,1)} async-done(((bf16[768,1536]{1,0:T(8,128)(2,1)}), bf16[3072,1536]{1,0:T(8,128)(2,1)}) %all-gather.15.cloned.1.call-update) | async-done | bytes 9437200 | tf_op jit(solution)/shard_map/all_gather | solution.py:194
  578.6 12.5 multiply_reduce_fusion.9
  645.4 70.8 %all-gather.19.cloned.1.call-done = bf16[384,64,128]{2,1,0:T(8,128)(2,1)} async-done(((bf16[48,64,128]{2,1,0:T(8,128)(2,1)}), bf16[384,64,128]{2,1,0:T(8,128)(2,1)}) %all-gather.19.cloned.1.call-update) | async-done | bytes 6291472 | tf_op jit(solution)/shard_map/all_gather | solution.py:53
  716.2 24.0 %while.81 = (s32[]{:T(128)}, f32[48,64,128]{2,1,0:T(8,128)}, s32[]{:T(128)}, bf16[8,48]{1,0:T(8,128)(2,1)S(1)}, bf16[8,48,64,128]{3,2,1,0:T(8,128)(2,1)}, /*index=5*/s32[]{:T(128)}, s32[]{:T(128)}, s32[]{:T(128)}, s32[]{:T(128)}) while((s32[]{:T(128)}, f32[48,64,128]{2,1,0:T(8,128)}, s32[]{:T(128)}, ...), condition=%wide.region_10.11_spmd.clone, body=%wide.region_9.10_spmd.clone.sunk | while | flops 1966136 | bytes 3932807 | solution.py:69
  749.2 248.0 %while.82 = (s32[]{:T(128)}, f32[48,64,128]{2,1,0:T(8,128)}, f32[48]{0:T(128)}, f32[2,256,48,64]{1,3,2,0:T(8,128)}, f32[2,256,128]{2,1,0:T(8,128)}, /*index=5*/f...) while((s32[]{:T(128)}, f32[48,64,128]{2,1,0:T(8,128)}, ...), condition=%wide.region_26.27_spmd.clone, body=%wide.region_13.26_spmd.clone.sunk | while | flops 11239392256 | bytes 115198616 | solution.py:125
  809.2 21.4 %fusion.264 = (f32[48,256]{1,0:T(8,128)S(1)}, f32[48,256]{1,0:T(8,128)S(1)}, f32[48,256]{1,0:T(8,128)}, f32[256,256]{1,0:T(8,128)}) fusion(f32[48,256]{1,0:T(8,128)S(1)} %bitcast.485, f32[256,256]{1,0:T(8,128)S(1)} %fusion.262, f32[48,256]{1,0:T(8,128)} %get-tuple-element.1593, pred[256,256]{1,0:T(8,128)(4,1)S(1)} %fusion.263, ...), kind=kOutput, calls=%fused_computation.72.clone.1 | convolution fusion | flops 2456711168 | bytes 7127040 | tf_op jit(solution)/shard_map/transpose(jvp())/while/body/eval_jaxpr/checkpoint/hts,shp->thp/dot_general | solution.py:88
  860.7 12.2 bitcast_dynamic-update-slice_fusion.7
  919.4 21.4 %fusion.264 = (f32[48,256]{1,0:T(8,128)S(1)}, f32[48,256]{1,0:T(8,128)S(1)}, f32[48,256]{1,0:T(8,128)}, f32[256,256]{1,0:T(8,128)}) fusion(f32[48,256]{1,0:T(8,128)S(1)} %bitcast.485, f32[256,256]{1,0:T(8,128)S(1)} %fusion.262, f32[48,256]{1,0:T(8,128)} %get-tuple-element.1593, pred[256,256]{1,0:T(8,128)(4,1)S(1)} %fusion.263, ...), kind=kOutput, calls=%fused_computation.72.clone.1 | convolution fusion | flops 2456711168 | bytes 7127040 | tf_op jit(solution)/shard_map/transpose(jvp())/while/body/eval_jaxpr/checkpoint/hts,shp->thp/dot_general | solution.py:88
  971.0 12.2 bitcast_dynamic-update-slice_fusion.7
  997.2 12.7 fusion.132
  1009.9 11.3 copy.299
  1075.3 16.4 convolution_convert_fusion
  1091.6 24.2 %copy.300 = bf16[1536,6448]{1,0:T(8,128)(2,1)} copy(bf16[1536,6448]{0,1:T(8,128)(2,1)} %convolution_convert_fusion) | data formatting | bytes 39616512
  1130.3 133.6 %reduce-scatter.10.cloned.1.call-done = bf16[384,6448]{1,0:T(8,128)(2,1)} async-done(((bf16[1536,6448]{1,0:T(8,128)(2,1)}), bf16[384,6448]{1,0:T(8,128)(2,1)}) %reduce-scatter.10.cloned.1.call-update) | async-done | bytes 4952080
  1271.5 74.1 %reduce-scatter.8.cloned.1.call-done = bf16[768,1536]{1,0:T(8,128)(2,1)} async-done(((bf16[3072,1536]{1,0:T(8,128)(2,1)}), bf16[768,1536]{1,0:T(8,128)(2,1)}) %reduce-scatter.8.cloned.1.call-update) | async-done | bytes 2359312 | tf_op jit(solution)/shard_map/reduce_scatter | solution.py:295
  1348.0 20.0 %fusion.135 = f32[512,1536]{1,0:T(8,128)S(1)} fusion(bf16[1536,6448]{0,1:T(8,128)(2,1)} %all-gather.13.cloned.1.call-done, bf16[512,48]{1,0:T(8,128)(2,1)S(1)} %copy-done.49, bf16[3,3328]{1,0:T(4,128)(2,1)S(1)} %fusion.147, bf16[509,3328]{1,0:T(8,128)(2,1)} %copy-done.19, bf16[512,3072]{1,0:T(8,128)(2,1)} %get-tuple-element.1247), kind=kOutput, calls=%fused_computation.222 | convolution fusion | flops 10168238080 | bytes 29556736 | tf_op jit(solution)/shard_map/dot_general | solution.py:281
  1368.1 12.7 multiply_reduce_fusion.15
  1382.2 44.0 %all-reduce.20 = (f32[48]{0:T(128)S(1)}, f32[48]{0:T(128)S(1)}, f32[48]{0:T(128)S(1)}, f32[2]{0:T(128)S(1)}) all-reduce(f32[48]{0:T(128)S(1)} %copy-done.80, f32[48]{0:T(128)S(1)} %fusion.156, f32[48]{0:T(128)S(1)} %reduce_sum.389, f32[2]{0:T(128)S(1)} %pad_maximum_fusion.3), channel_id=1, replica_groups=mesh['fsdp'=4,'ctx'=8] {'fsdp','ctx'}, use_global_device_ids=true, to_apply=%region_42.43 | all-reduce | flops 146 | bytes 1168 | tf_op jit(solution)/shard_map/psum | solution.py:320
  1427.9 11.9 all-reduce.23
  1440.0 21.3 %all-reduce.21 = (bf16[832]{0:T(1024)(128)(2,1)S(1)}, bf16[768]{0:T(1024)(128)(2,1)S(1)}, bf16[384]{0:T(512)(128)(2,1)S(1)}) all-reduce(bf16[832]{0:T(1024)(128)(2,1)S(1)} %dynamic-slice.5, bf16[768]{0:T(1024)(128)(2,1)S(1)} %dynamic-slice.7, bf16[384]{0:T(512)(128)(2,1)S(1)} %dynamic-slice.9), channel_id=1, replica_groups=mesh['fsdp'=4,'ctx'=8] {'ctx'}, use_global_device_ids=true, to_apply=%region_40.41 | all-reduce | flops 1984 | bytes 7936 | tf_op jit(solution)/shard_map/psum | solution.py:315
  1469.6 31.3 %all-gather.7 = bf16[8,832,4]{1,2,0:T(4,128)(2,1)S(1)} all-gather(bf16[1,832,4]{1,2,0:T(4,128)(2,1)S(1)} %bitcast.509), channel_id=4, replica_groups=mesh['fsdp'=4,'ctx'=8] {'ctx'}, dimensions={0}, use_global_device_ids=true | all-gather | bytes 59904 | tf_op jit(solution)/shard_map/all_gather | solution.py:20
  1501.5 119.0 %all-reduce.27.cloned.1.call-done = (bf16[384,6448]{0,1:T(8,128)(2,1)}, bf16[768,1536]{1,0:T(8,128)(2,1)}) async-done(((bf16[384,6448]{0,1:T(8,128)(2,1)}, bf16[768,1536]{1,0:T(8,128)(2,1)}), (bf16[384,6448]{0,1:T(8,128)(2,1)}, bf16[768,1536]{1,0:T(8,128)(2,1)})) %all-reduce.27.cloned.1.call-update) | async-done | bytes 7311376 | tf_op jit(solution)/shard_map/psum | solution.py:312
  (529 shorter events, 498.2 us)
Async XLA Ops:
  7.2 130.6 %all-gather.13.cloned.1.call-start = ((), (), s32[]{:S(2)}) async-start(), calls=%async_computation.3 | async-start | bytes 24760320 | tf_op jit(solution)/shard_map/all_gather | solution.py:183
  7.9 506.6 %all-gather.17.cloned.1.call-start = ((), (), s32[]{:S(2)}) async-start(), calls=%async_computation.6 | async-start | bytes 7077888 | tf_op jit(solution)/shard_map/all_gather | solution.py:33
  8.7 33.3 %collective-permute-start = (s32[3]{0:T(128)S(1)}, s32[3]{0:T(128)S(1)}, u32[]{:S(2)}, u32[]{:S(2)}) collective-permute-start(s32[3]{0:T(128)S(1)} %slice_bitcast_fusion), channel_id=1, source_target_pairs={{0,1},{1,2},{2,3},{3,4},{4,5},{5,6},{6,7},{8,9},{9,10},{10,11},{11... | collective-permute-start | bytes 44 | tf_op jit(solution)/shard_map/ppermute | solution.py:27
  19.5 135.0 %copy-start.65 = (f32[1536]{0:T(1024)}, f32[1536]{0:T(1024)S(1)}, u32[]{:S(2)}) copy-start(f32[1536]{0:T(1024)S(1)} %reshape.554) | copy-start | bytes 18436
  33.8 120.7 %copy-start.83 = (bf16[48]{0:T(256)(128)(2,1)}, bf16[48]{0:T(256)(128)(2,1)S(1)}, u32[]{:S(2)}) copy-start(bf16[48]{0:T(256)(128)(2,1)S(1)} %get-tuple-element.1205) | copy-start | bytes 292
  39.5 119.4 %copy-start.76 = (f32[48]{0:T(128)}, f32[48]{0:T(128)S(1)}, u32[]{:S(2)}) copy-start(f32[48]{0:T(128)S(1)} %convert_element_type.243) | copy-start | bytes 580
  41.5 126.0 %copy-start.40 = (f32[3328]{0:T(1024)}, f32[3328]{0:T(1024)S(1)}, u32[]{:S(2)}) copy-start(f32[3328]{0:T(1024)S(1)} %get-tuple-element.1104) | copy-start | bytes 39940
  41.5 126.0 %copy-start.42 = (f32[3328]{0:T(1024)}, f32[3328]{0:T(1024)S(1)}, u32[]{:S(2)}) copy-start(f32[3328]{0:T(1024)S(1)} %get-tuple-element.1105) | copy-start | bytes 39940
  41.6 126.0 %copy-start.44 = (f32[3328]{0:T(1024)}, f32[3328]{0:T(1024)S(1)}, u32[]{:S(2)}) copy-start(f32[3328]{0:T(1024)S(1)} %get-tuple-element.1106) | copy-start | bytes 39940
  41.6 126.0 %copy-start.46 = (f32[3328]{0:T(1024)}, f32[3328]{0:T(1024)S(1)}, u32[]{:S(2)}) copy-start(f32[3328]{0:T(1024)S(1)} %get-tuple-element.1107) | copy-start | bytes 39940
  42.0 117.0 %copy-start.78 = (f32[48]{0:T(128)}, f32[48]{0:T(128)S(1)}, u32[]{:S(2)}) copy-start(f32[48]{0:T(128)S(1)} %convert_exponential_fusion) | copy-start | bytes 580
  42.0 112.5 %copy-start.73 = (f32[512]{0:T(512)}, f32[512]{0:T(512)S(1)}, u32[]{:S(2)}) copy-start(f32[512]{0:T(512)S(1)} %add_rsqrt_fusion) | copy-start | bytes 6148
  44.6 123.0 %copy-start.59 = (f32[512]{0:T(512)}, f32[512]{0:T(512)S(1)}, u32[]{:S(2)}) copy-start(f32[512]{0:T(512)S(1)} %get-tuple-element.1258) | copy-start | bytes 6148
  44.6 123.0 %copy-start.61 = (f32[512]{0:T(512)}, f32[512]{0:T(512)S(1)}, u32[]{:S(2)}) copy-start(f32[512]{0:T(512)S(1)} %get-tuple-element.1259) | copy-start | bytes 6148
  44.6 123.0 %copy-start.63 = (f32[512]{0:T(512)}, f32[512]{0:T(512)S(1)}, u32[]{:S(2)}) copy-start(f32[512]{0:T(512)S(1)} %get-tuple-element.1260) | copy-start | bytes 6148
  155.3 9.5 collective-permute-start.1
  205.0 212.5 %copy-start.81 = (bf16[768]{0:T(1024)(128)(2,1)S(1)}, bf16[768]{0:T(1024)(128)(2,1)}, u32[]{:S(2)}) copy-start(bf16[768]{0:T(1024)(128)(2,1)} %param.30) | copy-start | bytes 4612
  416.2 162.4 %all-gather.15.cloned.1.call-start = ((), (), s32[]{:S(2)}) async-start(), calls=%async_computation.4 | async-start | bytes 11796480 | tf_op jit(solution)/shard_map/all_gather | solution.py:194
  416.9 299.3 %all-gather.19.cloned.1.call-start = ((), (), s32[]{:S(2)}) async-start(), calls=%async_computation.7 | async-start | bytes 7077888 | tf_op jit(solution)/shard_map/all_gather | solution.py:53
  422.7 168.4 %copy-start.55 = (f32[4,1,768]{2,1,0:T(1,128)}, f32[4,1,768]{2,1,0:T(1,128)S(1)}, u32[]{:S(2)}) copy-start(f32[4,1,768]{2,1,0:T(1,128)S(1)} %convert_element_type.283) | copy-start | bytes 36868
  452.6 156.2 %copy-start.24 = (f32[512,48]{0,1:T(8,128)}, f32[512,48]{0,1:T(8,128)S(1)}, u32[]{:S(2)}) copy-start(f32[512,48]{0,1:T(8,128)S(1)} %exponential_multiply_fusion.4) | copy-start | bytes 294916
  514.7 225.5 %copy-start.2 = (f32[48,64,128]{2,1,0:T(8,128)}, f32[48,64,128]{2,1,0:T(8,128)S(1)}, u32[]{:S(2)}) copy-start(f32[48,64,128]{2,1,0:T(8,128)S(1)} %get-tuple-element.688) | copy-start | bytes 4718596
  617.1 646.9 %reduce-scatter.10.cloned.1.call-start = ((), (), s32[]{:S(2)}) async-start(), calls=%async_computation.8 | async-start | bytes 25067520
  1065.7 7.9 collective-permute-start.2
  1115.9 229.8 %reduce-scatter.8.cloned.1.call-start = ((), (), s32[]{:S(2)}) async-start(), calls=%async_computation.5 | async-start | bytes 11796480 | tf_op jit(solution)/shard_map/reduce_scatter | solution.py:295
  1128.5 340.1 %reduce-scatter.12.cloned.1.call-start = ((), (), s32[]{:S(2)}) async-start(), calls=%async_computation.9 | async-start | bytes 1064960
  1130.0 217.8 %copy-start.57 = (f32[3072]{0:T(1024)S(1)}, f32[3072]{0:T(1024)}, u32[]{:S(2)}) copy-start(f32[3072]{0:T(1024)} %get-tuple-element.1210) | copy-start | bytes 36868
  1130.0 218.0 %copy-start.82 = (f32[48]{0:T(128)S(1)}, f32[48]{0:T(128)}, u32[]{:S(2)}) copy-start(f32[48]{0:T(128)} %get-tuple-element.1248) | copy-start | bytes 580
  1130.0 218.0 %copy-start.84 = (bf16[48]{0:T(256)(128)(2,1)S(1)}, bf16[48]{0:T(256)(128)(2,1)}, u32[]{:S(2)}) copy-start(bf16[48]{0:T(256)(128)(2,1)} %copy-done.83) | copy-start | bytes 292
  1130.0 218.0 %copy-start.49 = (bf16[512,48]{1,0:T(8,128)(2,1)S(1)}, bf16[512,48]{1,0:T(8,128)(2,1)}, u32[]{:S(2)}) copy-start(bf16[512,48]{1,0:T(8,128)(2,1)} %copy-done.48) | copy-start | bytes 147460
  1130.0 490.5 %all-reduce.27.cloned.1.call-start = ((), (), s32[]{:S(2)}) async-start(), calls=%async_computation.10 | async-start | bytes 14622720 | tf_op jit(solution)/shard_map/psum | solution.py:312
  1368.1 59.8 %copy-start.75 = (bf16[3072]{0:T(1024)(128)(2,1)S(1)}, bf16[3072]{0:T(1024)(128)(2,1)}, u32[]{:S(2)}) copy-start(bf16[3072]{0:T(1024)(128)(2,1)} %get-tuple-element.1095) | copy-start | bytes 18436
  (98 other events, 1464.4 us)
Sparse Core Ops, SparseCore 0:
  9.6 128.1 all-gather.12
  416.3 98.1 all-gather.16
  516.1 62.4 all-gather.14
  617.2 99.0 all-gather.18
  1116.0 147.9 reduce-scatter.9
  1267.2 78.4 reduce-scatter.7
  1348.4 23.6 reduce-scatter.11
  1376.1 244.3 all-reduce.26
